TPU v7x, 512 devices: a whole 4x8x8 slice. The times are simulated.
512 devices in a mesh: dom: 16 (over z_hi, y), rel: 32 (over z_lo, x, core).
Axes of the slice: x: 4, y: 8, z: 8 (z_hi: 2, z_lo: 4; z = z_hi * 4 + z_lo), core: 2. Of those that a mesh axis runs over, the one named last changes fastest.
Arguments:
- entity: float32 [65536, 512], P(('dom', 'rel')), may hold values from -1.8 to 1.8
- entity_acc: float32 [65536, 512], P(('dom', 'rel')), may hold values from 0.01 to 1
- relation: float32 [4096, 512], P('rel'), may hold values from -1 to 1, as said below
- relation_acc: float32 [4096, 512], P('rel'), may hold values from 0.01 to 1
- send_rows: int32 [512, 32, 16], P(('dom', 'rel')), may hold values from 0 to 127, as said below
- trip_head: int32 [131072], P(('dom', 'rel')), may hold values from 0 to 511
- trip_rel: int32 [131072], P(('dom', 'rel')), may hold values from 0 to 127
- trip_tail: int32 [131072], P(('dom', 'rel')), may hold values from 0 to 511
- neg_part: int32 [1], replicated, may hold values from 0 to 15
- neg_rows: int32 [32, 32], replicated, may hold values from 0 to 127
Outputs:
- new_entity: float32 [65536, 512], P(('dom', 'rel'))
- new_entity_acc: float32 [65536, 512], P(('dom', 'rel'))
- new_relation: float32 [4096, 512], P('rel')
- new_relation_acc: float32 [4096, 512], P('rel')
Inputs may be any that keep to these rules, and one draw needn't show every extreme that they name: `send_rows`: within one owner's list for one receiver the 16 rows are distinct. `relation`: every component has magnitude 0.1 or more.
All inputs are finite; a program needn't handle non-finite values.
Results may differ from a plain program's by a relative error of at most 0.0003.
Values sent between devices are 32-bit elements; how exact they have to be, the bound alone decides.
A program may use at most 64 MiB of HBM per device.

v0:
```python
import jax
import jax.numpy as jnp
from jax import lax
from jax.sharding import PartitionSpec as P

step_size = 0.05


def broadcast(block, axis, owner):
    block = jnp.where(lax.axis_index(axis) == owner, block, jnp.zeros_like(block))
    return lax.psum(block, axis)


def hamilton(left, right):
    left_a, left_b, left_c, left_d = jnp.split(left, 4, axis=-1)
    right_a, right_b, right_c, right_d = jnp.split(right, 4, axis=-1)
    out_a = left_a * right_a - left_b * right_b - left_c * right_c - left_d * right_d
    out_b = left_a * right_b + left_b * right_a + left_c * right_d - left_d * right_c
    out_c = left_a * right_c - left_b * right_d + left_c * right_a + left_d * right_b
    out_d = left_a * right_d + left_b * right_c - left_c * right_b + left_d * right_a
    return jnp.concatenate([out_a, out_b, out_c, out_d], axis=-1)


def unit_rel(relation):
    comp_a, comp_b, comp_c, comp_d = jnp.split(relation, 4, axis=-1)
    magnitude = jnp.sqrt(comp_a * comp_a + comp_b * comp_b + comp_c * comp_c + comp_d * comp_d)
    return relation / jnp.concatenate([magnitude, magnitude, magnitude, magnitude], axis=-1)


def local_loss(touched, relation, negatives, heads, rels, tails):
    unit_rows = unit_rel(relation)
    one_hot = (rels[:, None] == jnp.arange(relation.shape[0])[None, :]).astype(unit_rows.dtype)
    rotation = jnp.dot(one_hot, unit_rows, precision=lax.Precision.HIGHEST)
    query = hamilton(touched[heads], rotation)
    positive = jnp.sum(query * touched[tails], axis=-1)
    scores = jnp.einsum("ik,jk->ij", query, negatives, precision=lax.Precision.HIGHEST)
    return (
        jnp.sum(jax.nn.softplus(-positive)) + jnp.sum(jax.nn.softplus(scores)) / negatives.shape[0]
    )


def adagrad(values, history, gradient):
    history_new = history + gradient * gradient
    return (values - step_size * gradient / jnp.sqrt(history_new), history_new)


def shards(
    entity,
    entity_acc,
    relation,
    relation_acc,
    send_rows,
    trip_head,
    trip_rel,
    trip_tail,
    neg_part,
    neg_rows,
):
    row_width = entity.shape[1]
    send_lists = send_rows[0]
    outgoing = entity[send_lists]
    touched = lax.all_to_all(outgoing, "rel", split_axis=0, concat_axis=0, tiled=True).reshape(
        -1, row_width
    )
    neg_root = neg_part[0]
    rel_here = lax.axis_index("rel")
    own_negs = entity[neg_rows[rel_here]]
    grouped = lax.all_gather(own_negs, "rel", axis=0, tiled=True)
    negatives = broadcast(grouped, "dom", neg_root)

    def scored(touched_in, relation_in, negatives_in):
        return local_loss(touched_in, relation_in, negatives_in, trip_head, trip_rel, trip_tail)

    loss_value, pullback = jax.vjp(scored, touched, relation, negatives)
    grad_rows, grad_rel, grad_neg = pullback(jnp.ones_like(loss_value))
    returned = lax.all_to_all(
        grad_rows.reshape(-1, send_lists.shape[1], row_width),
        "rel",
        split_axis=0,
        concat_axis=0,
        tiled=True,
    )
    ent_grad = jnp.zeros_like(entity).at[send_lists].add(returned)
    neg_share = lax.psum_scatter(grad_neg, "rel", scatter_dimension=0, tiled=True)
    neg_total = lax.psum(neg_share, "dom")
    is_owner = (lax.axis_index("dom") == neg_root).astype(jnp.float32)
    ent_grad = ent_grad.at[neg_rows[rel_here]].add(is_owner * neg_total)
    new_entity, new_entity_acc = adagrad(entity, entity_acc, ent_grad)
    rel_sum = lax.psum(grad_rel, "dom")
    new_relation, new_relation_acc = adagrad(relation, relation_acc, rel_sum)
    return (new_entity, new_entity_acc, new_relation, new_relation_acc)


def solution(mesh):
    in_specs = (
        P(("dom", "rel"), None),
        P(("dom", "rel"), None),
        P("rel", None),
        P("rel", None),
        P(("dom", "rel"), None, None),
        P(("dom", "rel")),
        P(("dom", "rel")),
        P(("dom", "rel")),
        P(),
        P(),
    )
    out_specs = (P(("dom", "rel"), None), P(("dom", "rel"), None), P("rel", None), P("rel", None))
    return jax.shard_map(shards, mesh=mesh, in_specs=in_specs, out_specs=out_specs, check_vma=False)
```

profile of v0, /device:TPU:8, one launch (start us, length us, event | category | flops | bytes accessed | tf_op | source)
XLA Modules:
  0.0 652.1 jit_solution(494855978399194900)
XLA Ops:
  7.2 0.7 fusion.40
  8.0 2.2 gather_fusion.3
  10.2 0.7 compare_select_fusion.3
  11.1 2.3 gather_fusion
  13.4 10.1 %all-to-all-start = ((f32[32,16,512]{2,1,0:T(8,128)}), f32[32,16,512]{2,1,0:T(8,128)S(1)}, u32[]{:S(2)}, u32[]{:S(2)}) async-start(f32[32,16,512]{2,1,0:T(8,128)} %bitcast.1), calls=%async_computation | async-start | bytes 2097152 | tf_op jit(solution)/shard_map/all_to_all | solution.py:62
  24.2 57.4 %all-gather.3.cloned.1.call-done = f32[1024,512]{1,0:T(8,128)} async-done(((f32[32,512]{1,0:T(8,128)}), f32[1024,512]{1,0:T(8,128)}) %all-gather.3.cloned.1.call-update) | async-done | bytes 2097168 | tf_op jit(solution)/shard_map/all_gather | solution.py:68
  81.6 1.6 broadcast_select_fusion
  83.3 0.6 copy-done.12
  83.9 0.3 copy-done.1
  84.2 0.4 fusion.24
  84.7 0.2 copy-done.10
  84.8 1.0 gather_fusion.1
  86.0 205.6 %all-reduce.4.cloned.1.call-done = f32[1024,512]{1,0:T(8,128)} async-done(((f32[1024,512]{1,0:T(8,128)}), f32[1024,512]{1,0:T(8,128)}) %all-reduce.4.cloned.1.call-update) | async-done | bytes 2097168 | tf_op jit(solution)/shard_map/psum | solution.py:11
  291.6 3.5 fusion.49
  295.1 1.0 copy-done.7
  296.1 3.9 fusion.28
  300.0 0.7 copy-done.13
  300.7 1.0 gather_fusion.2
  301.7 0.1 multiply_reduce_fusion
  301.8 0.7 copy-done.3
  302.5 3.1 scatter_custom_fusion
  305.6 4.7 convolution_add_fusion
  310.5 3.1 scatter_custom_fusion.1
  313.7 2.4 add_any.115
  316.1 5.3 all-to-all-start.1
  321.7 0.4 multiply_negate_fusion
  322.2 0.7 maximum_add_fusion
  322.9 127.9 %reduce-scatter.2.cloned.1.call-done = f32[32,512]{1,0:T(8,128)} async-done(((f32[1024,512]{1,0:T(8,128)}), f32[32,512]{1,0:T(8,128)}) %reduce-scatter.2.cloned.1.call-update) | async-done | bytes 65552 | tf_op jit(solution)/shard_map/reduce_scatter | solution.py:84
  450.9 3.6 scatter_custom_fusion.2
  454.5 187.9 %all-reduce.6.cloned.1.call-done = (f32[32,512]{1,0:T(8,128)}, f32[128,512]{1,0:T(8,128)}) async-done(((f32[32,512]{1,0:T(8,128)}, f32[128,512]{1,0:T(8,128)}), (f32[32,512]{1,0:T(8,128)}, f32[128,512]{1,0:T(8,128)})) %all-reduce.6.cloned.1.call-update) | async-done | bytes 327696 | tf_op jit(solution)/shard_map/psum | solution.py:85
  642.4 1.2 scatter_custom_fusion.3
  643.6 2.0 multiply_subtract_fusion
  (54 shorter events, 1.1 us)
Async XLA Ops:
  7.2 3.9 copy-start
  7.2 74.5 %all-gather.3.cloned.1.call-start = ((), (), s32[]{:S(2)}) async-start(), calls=%async_computation.5 | async-start | bytes 2162688 | tf_op jit(solution)/shard_map/all_gather | solution.py:68
  13.4 71.3 %all-to-all-start = ((f32[32,16,512]{2,1,0:T(8,128)}), f32[32,16,512]{2,1,0:T(8,128)S(1)}, u32[]{:S(2)}, u32[]{:S(2)}) async-start(f32[32,16,512]{2,1,0:T(8,128)} %bitcast.1), calls=%async_computation | async-start | bytes 2097152 | tf_op jit(solution)/shard_map/all_to_all | solution.py:62
  23.5 268.0 %all-reduce.4.cloned.1.call-start = ((), (), s32[]{:S(2)}) async-start(), calls=%async_computation.3 | async-start | bytes 4194304 | tf_op jit(solution)/shard_map/psum | solution.py:11
  83.2 0.7 copy-start.12
  83.2 1.0 copy-start.1
  83.2 1.0 copy-start.14
  83.2 367.6 %reduce-scatter.2.cloned.1.call-start = ((), (), s32[]{:S(2)}) async-start(), calls=%async_computation.4 | async-start | bytes 2162688 | tf_op jit(solution)/shard_map/reduce_scatter | solution.py:84
  84.2 0.6 copy-start.10
  85.9 215.8 %copy-start.4 = (f32[256,128]{1,0:T(8,128)}, f32[256,128]{1,0:T(8,128)S(1)}, u32[]{:S(2)}) copy-start(f32[256,128]{1,0:T(8,128)S(1)} %get-tuple-element.23) | copy-start | bytes 393220
  86.0 215.7 %copy-start.5 = (f32[256,128]{1,0:T(8,128)}, f32[256,128]{1,0:T(8,128)S(1)}, u32[]{:S(2)}) copy-start(f32[256,128]{1,0:T(8,128)S(1)} %get-tuple-element.20) | copy-start | bytes 393220
  86.0 215.7 %copy-start.6 = (f32[256,128]{1,0:T(8,128)}, f32[256,128]{1,0:T(8,128)S(1)}, u32[]{:S(2)}) copy-start(f32[256,128]{1,0:T(8,128)S(1)} %get-tuple-element.21) | copy-start | bytes 393220
  295.1 1.0 copy-start.7
  300.0 0.7 copy-start.13
  301.7 0.8 copy-start.3
  316.1 5.6 copy-start.2
  316.1 5.6 copy-start.11
  316.1 5.6 copy-start.15
  316.1 134.8 %all-to-all-start.1 = ((f32[32,16,512]{2,1,0:T(8,128)}), f32[32,16,512]{2,1,0:T(8,128)S(1)}, u32[]{:S(2)}, u32[]{:S(2)}) async-start(f32[32,16,512]{2,1,0:T(8,128)} %bitcast.6), calls=%async_computation.1 | async-start | bytes 2097152 | tf_op jit(solution)/shard_map/all_to_all | solution.py:76
  321.4 321.0 %all-reduce.6.cloned.1.call-start = ((), (), s32[]{:S(2)}) async-start(), calls=%async_computation.6 | async-start | bytes 655360 | tf_op jit(solution)/shard_map/psum | solution.py:85
  321.7 321.9 %copy-start.8 = (f32[128,512]{1,0:T(8,128)S(1)}, f32[128,512]{1,0:T(8,128)}, u32[]{:S(2)}) copy-start(f32[128,512]{1,0:T(8,128)} %param.13) | copy-start | bytes 786436
  321.7 321.9 %copy-start.9 = (f32[128,512]{1,0:T(8,128)S(1)}, f32[128,512]{1,0:T(8,128)}, u32[]{:S(2)}) copy-start(f32[128,512]{1,0:T(8,128)} %param.11) | copy-start | bytes 786436
Sparse Core Ops, SparseCore 0:
  10.7 70.8 all-gather.2
  84.6 206.9 all-reduce.3
  300.1 150.6 reduce-scatter.1
  454.3 188.0 all-reduce.5
where the time goes:
time: 653 us; the launch traced here: 652 us
  waiting for transfers between devices  579 us (89%)
  other arithmetic  20 us (3%)
  starting transfers between devices  15.6 us (2%)
  between operations  14.7 us (2%)
  matrix products  13 us (2%)
  local copies, waits for them, and re-layouts  10.1 us (2%)
    psum x1, waiting for transfers between devices, broadcast(): return lax.psum(block, axis)  206 us
    psum x1, waiting for transfers between devices, shards(): neg_total = lax.psum(neg_share, 'dom')  188 us
    reduce_scatter x1, waiting for transfers between devices, shards(): lax.psum_scatter(grad_neg, 'rel', scatter_dimension=0, tiled=True)  128 us
    all_gather x1, waiting for transfers between devices, shards(): grouped = lax.all_gather(own_negs, 'rel', axis=0, tiled=True)  57.4 us
  transfers between devices with their start and end apart: 6, of which 4 were waited for; matrix products, arithmetic and copies ran while one was open for 4% of the time, Pallas kernels for 0%

commit v1 on v0

--- a/solution.py
+++ b/solution.py
@@ -8,7 +8,7 @@
 
 def broadcast(block, axis, owner):
     block = jnp.where(lax.axis_index(axis) == owner, block, jnp.zeros_like(block))
-    return lax.psum(block, axis)
+    return jnp.sum(lax.all_gather(block, axis), axis=0)
 
 
 def hamilton(left, right):

time: 653 us -> 1090 us (1.67)
  waiting for transfers between devices: 579 us -> 1010 us
  other arithmetic: 20 us -> 33.2 us
    all_gather x0 -> x1, waiting for transfers between devices: none -> 555 us  [broadcast(): return jnp.sum(lax.all_gather(block, axis), axis=0)]
    psum x1 -> x0, waiting for transfers between devices: 206 us -> none  [broadcast(): return lax.psum(block, axis)]
    all_to_all x1, waiting for transfers between devices: 0.01 us -> 70.6 us  [shards(): lax.all_to_all(outgoing, 'rel', split_axis=0, concat_axis=0, tiled=True)]
    reduce_sum x0 -> x1, other arithmetic: none -> 14 us  [broadcast(): return jnp.sum(lax.all_gather(block, axis), axis=0)]
  transfers between devices with their start and end apart: 6 -> 6, of which waited for: 4 -> 5; matrix products, arithmetic and copies ran while one was open for 4% -> 2% of each run, Pallas kernels for 0% -> 0%
where the time goes in v1:
time: 1090 us
  waiting for transfers between devices  1010 us (93%)
  other arithmetic  33.2 us (3%)
  between operations  14.8 us (1%)
  matrix products  12.3 us (1%)
  local copies, waits for them, and re-layouts  11 us (1%)
    all_gather x1, waiting for transfers between devices, broadcast(): return jnp.sum(lax.all_gather(block, axis), axis=0)  555 us
    psum x1, waiting for transfers between devices, shards(): neg_total = lax.psum(neg_share, 'dom')  188 us
    reduce_scatter x1, waiting for transfers between devices, shards(): lax.psum_scatter(grad_neg, 'rel', scatter_dimension=0, tiled=True)  126 us
    all_to_all x1, waiting for transfers between devices, shards(): lax.all_to_all(outgoing, 'rel', split_axis=0, concat_axis=0, tiled=True)  70.6 us
    all_gather x1, waiting for transfers between devices, shards(): grouped = lax.all_gather(own_negs, 'rel', axis=0, tiled=True)  66.8 us
  transfers between devices with their start and end apart: 6, of which 5 were waited for; matrix products, arithmetic and copies ran while one was open for 2% of the time, Pallas kernels for 0%

profile of v1, /device:TPU:8, one launch (start us, length us, event | category | flops | bytes accessed | tf_op | source)
XLA Modules:
  0.0 1088.0 jit_solution(16946602358131385647)
XLA Ops:
  7.2 0.7 fusion.40
  7.9 0.5 copy-done.18
  8.5 2.2 gather_fusion.3
  11.4 66.8 %all-gather.5.cloned.1.call-done = f32[1024,512]{1,0:T(8,128)} async-done(((f32[32,512]{1,0:T(8,128)}), f32[1024,512]{1,0:T(8,128)}) %all-gather.5.cloned.1.call-update) | async-done | bytes 2097168 | tf_op jit(solution)/shard_map/all_gather | solution.py:68
  78.2 1.5 broadcast_select_fusion
  79.7 0.7 copy-done.15
  80.7 2.3 gather_fusion
  83.0 5.4 all-to-all-start
  88.6 0.4 fusion.24
  89.0 70.6 %all-to-all-done = f32[32,16,512]{2,1,0:T(8,128)S(1)} async-done(((f32[32,16,512]{2,1,0:T(8,128)}), f32[32,16,512]{2,1,0:T(8,128)S(1)}, u32[]{:S(2)}, u32[]{:S(2)}) %all-to-all-start) | async-done | bytes 1048608 | tf_op jit(solution)/shard_map/all_to_all | solution.py:62
  159.6 1.0 gather_fusion.1
  160.8 555.0 %all-gather.7.cloned.1.call-done = f32[16384,512]{1,0:T(8,128)} async-done(((f32[1024,512]{1,0:T(8,128)}), f32[16384,512]{1,0:T(8,128)}) %all-gather.7.cloned.1.call-update) | async-done | bytes 33554448 | tf_op jit(solution)/shard_map/all_gather | solution.py:11
  715.7 14.0 %reduce_sum.19 = f32[1024,512]{1,0:T(8,128)} reduce(f32[16,1024,512]{2,1,0:T(8,128)} %bitcast.19, f32[]{:T(128)} %constant.13.clone.1), dimensions={0}, to_apply=%region_2.3 | reduce | flops 7864320 | bytes 35651588 | tf_op jit(solution)/shard_map/reduce_sum | solution.py:11
  729.7 3.5 fusion.49
  733.3 1.0 copy-done.10
  734.3 3.9 fusion.28
  738.2 0.7 copy-done.17
  738.9 1.8 gather_fusion.2
  740.7 1.4 multiply_reduce_fusion
  742.1 3.7 scatter_custom_fusion
  745.8 4.1 convolution_add_fusion
  750.1 0.6 copy-done.2
  750.7 2.4 scatter_custom_fusion.1
  753.1 1.2 add_any.115
  754.3 4.8 all-to-all-start.1
  759.4 0.4 multiply_negate_fusion
  759.9 0.7 maximum_add_fusion
  760.6 125.8 %reduce-scatter.2.cloned.1.call-done = f32[32,512]{1,0:T(8,128)} async-done(((f32[1024,512]{1,0:T(8,128)}), f32[32,512]{1,0:T(8,128)}) %reduce-scatter.2.cloned.1.call-update) | async-done | bytes 65552 | tf_op jit(solution)/shard_map/reduce_scatter | solution.py:84
  886.4 3.6 scatter_custom_fusion.2
  890.1 188.2 %all-reduce.3.cloned.1.call-done = (f32[32,512]{1,0:T(8,128)}, f32[128,512]{1,0:T(8,128)}) async-done(((f32[32,512]{1,0:T(8,128)}, f32[128,512]{1,0:T(8,128)}), (f32[32,512]{1,0:T(8,128)}, f32[128,512]{1,0:T(8,128)})) %all-reduce.3.cloned.1.call-update) | async-done | bytes 327696 | tf_op jit(solution)/shard_map/psum | solution.py:85
  1078.2 1.2 scatter_custom_fusion.3
  1079.5 2.0 multiply_subtract_fusion
  (65 shorter events, 1.2 us)
Async XLA Ops:
  7.2 71.0 %all-gather.5.cloned.1.call-start = ((), (), s32[]{:S(2)}) async-start(), calls=%async_computation.4 | async-start | bytes 2162688 | tf_op jit(solution)/shard_map/all_gather | solution.py:68
  7.9 0.5 copy-start.18
  10.7 705.0 %all-gather.7.cloned.1.call-start = ((), (), s32[]{:S(2)}) async-start(), calls=%async_computation.5 | async-start | bytes 35651584 | tf_op jit(solution)/shard_map/all_gather | solution.py:11
  79.7 0.7 copy-start.15
  79.7 1.0 copy-start
  83.0 5.5 copy-start.16
  83.0 5.5 copy-start.5
  83.0 5.6 copy-start.19
  83.0 76.6 %all-to-all-start = ((f32[32,16,512]{2,1,0:T(8,128)}), f32[32,16,512]{2,1,0:T(8,128)S(1)}, u32[]{:S(2)}, u32[]{:S(2)}) async-start(f32[32,16,512]{2,1,0:T(8,128)} %bitcast.1), calls=%async_computation | async-start | bytes 2097152 | tf_op jit(solution)/shard_map/all_to_all | solution.py:62
  88.4 798.0 %reduce-scatter.2.cloned.1.call-start = ((), (), s32[]{:S(2)}) async-start(), calls=%async_computation.3 | async-start | bytes 2162688 | tf_op jit(solution)/shard_map/reduce_scatter | solution.py:84
  88.6 71.0 %copy-start.13 = (f32[128,128]{1,0:T(8,128)}, f32[128,128]{1,0:T(8,128)S(1)}, u32[]{:S(2)}) copy-start(f32[128,128]{1,0:T(8,128)S(1)} %add_sqrt_fusion) | copy-start | bytes 196612
  160.6 572.6 %copy-start.7 = (f32[256,128]{1,0:T(8,128)}, f32[256,128]{1,0:T(8,128)S(1)}, u32[]{:S(2)}) copy-start(f32[256,128]{1,0:T(8,128)S(1)} %get-tuple-element.23) | copy-start | bytes 393220
  160.7 572.5 %copy-start.8 = (f32[256,128]{1,0:T(8,128)}, f32[256,128]{1,0:T(8,128)S(1)}, u32[]{:S(2)}) copy-start(f32[256,128]{1,0:T(8,128)S(1)} %get-tuple-element.20) | copy-start | bytes 393220
  160.7 572.5 %copy-start.9 = (f32[256,128]{1,0:T(8,128)}, f32[256,128]{1,0:T(8,128)S(1)}, u32[]{:S(2)}) copy-start(f32[256,128]{1,0:T(8,128)S(1)} %get-tuple-element.21) | copy-start | bytes 393220
  733.3 1.0 copy-start.10
  738.2 0.7 copy-start.17
  740.7 5.1 copy-start.1
  749.9 0.8 copy-start.2
  749.9 3.2 copy-start.4
  753.1 6.1 copy-start.3
  754.3 5.0 copy-start.6
  754.3 5.0 copy-start.14
  754.3 5.0 copy-start.20
  754.3 132.1 %all-to-all-start.1 = ((f32[32,16,512]{2,1,0:T(8,128)}), f32[32,16,512]{2,1,0:T(8,128)S(1)}, u32[]{:S(2)}, u32[]{:S(2)}) async-start(f32[32,16,512]{2,1,0:T(8,128)} %bitcast.7), calls=%async_computation.1 | async-start | bytes 2097152 | tf_op jit(solution)/shard_map/all_to_all | solution.py:76
  759.1 319.1 %all-reduce.3.cloned.1.call-start = ((), (), s32[]{:S(2)}) async-start(), calls=%async_computation.6 | async-start | bytes 655360 | tf_op jit(solution)/shard_map/psum | solution.py:85
  759.4 320.1 %copy-start.11 = (f32[128,512]{1,0:T(8,128)S(1)}, f32[128,512]{1,0:T(8,128)}, u32[]{:S(2)}) copy-start(f32[128,512]{1,0:T(8,128)} %param.13) | copy-start | bytes 786436
  759.4 320.1 %copy-start.12 = (f32[128,512]{1,0:T(8,128)S(1)}, f32[128,512]{1,0:T(8,128)}, u32[]{:S(2)}) copy-start(f32[128,512]{1,0:T(8,128)} %param.11) | copy-start | bytes 786436
Sparse Core Ops, SparseCore 0:
  10.8 67.3 all-gather.4
  81.4 634.3 all-gather.6
  738.4 147.9 reduce-scatter.1
  889.8 188.3 all-reduce.2
